TPU v7x, 256 devices: a whole 4x4x8 slice. The times are simulated.
256 devices in a mesh: tm: 4 (over z_lo, core), firm: 64 (over y, x, z_hi).
Axes of the slice: x: 4, y: 4, z: 8 (z_hi: 4, z_lo: 2; z = z_hi * 2 + z_lo), core: 2. Of those that a mesh axis runs over, the one named last changes fastest.
Arguments:
- features: bfloat16 [32, 16384, 256], P('tm', 'firm'), may hold values from -6 to 6
- supply_counts: int32 [32, 16384, 3, 256], P('tm', 'firm'), may hold values from 0 to 3
- bank_ids: int32 [32, 16384], P('tm', 'firm'), may hold values from 0 to 511
- sector_ids: int32 [32, 16384], P('tm', 'firm'), may hold values from 0 to 255
- bank_table: bfloat16 [512, 256], P('firm'), may hold values from -6 to 6
- sector_table: bfloat16 [256, 256], P('firm'), may hold values from -6 to 6
- w_supply: bfloat16 [256, 256], replicated, may hold values from -0.375 to 0.375
- w_query: bfloat16 [256, 256], replicated, may hold values from -0.375 to 0.375
- w_key: bfloat16 [256, 256], replicated, may hold values from -0.375 to 0.375
- w_value: bfloat16 [256, 256], replicated, may hold values from -0.375 to 0.375
- w_out: bfloat16 [256, 256], replicated, may hold values from -0.375 to 0.375
- w_in: bfloat16 [256, 1024], replicated, may hold values from -0.375 to 0.375
- w_down: bfloat16 [1024, 256], replicated, may hold values from -0.1875 to 0.1875
- gain_mix: float32 [256], replicated, may hold values from 0.1 to 1.9
- gain_ffn: float32 [256], replicated, may hold values from 0.1 to 1.9
Outputs:
- result: bfloat16 [32, 16384, 256], P('tm', 'firm')
All inputs are finite; a program needn't handle non-finite values.
Results may differ from a plain program's by a relative error of at most 0.0059.
Values may be sent and summed in bfloat16 or wider, within the bound.
No kernel may reach another device: no remote copies, remote signals or barrier semaphores. Data moves between devices by JAX's collectives and lax.ppermute only.
A program may use at most 64 MiB of HBM per device.

v0:
```python
import jax
import jax.numpy as jnp
from jax import lax
from jax.sharding import PartitionSpec as P

HEADS = 4


def padded(x, sides, width):
    for axis, dim in sides:
        devices, length = (lax.axis_size(axis), x.shape[dim])
        up = [(i, (i + 1) % devices) for i in range(devices - 1)]
        down = [(j, i) for i, j in up]
        last = lax.slice_in_dim(x, length - width, length, axis=dim)
        leading = lax.slice_in_dim(x, 0, width, axis=dim)
        before = lax.ppermute(last, axis, up)
        after = lax.ppermute(leading, axis, down)
        x = jnp.concatenate([before, x, after], axis=dim)
    return x


def from_behind(x, axis, by):
    devices = lax.axis_size(axis)
    pairs = [(i, i + by) for i in range(devices) if 0 <= i + by < devices]
    return lax.ppermute(x, axis, pairs)


def rms_norm(values, gain):
    scale = lax.rsqrt(jnp.mean(values * values, axis=-1, keepdims=True) + 1e-06)
    return values * scale * gain


def body(
    features,
    supply_counts,
    bank_ids,
    sector_ids,
    bank_table,
    sector_table,
    w_supply,
    w_query,
    w_key,
    w_value,
    w_out,
    w_in,
    w_down,
    gain_mix,
    gain_ffn,
):
    months, firms, width = features.shape
    rows = months * firms
    flat = features.reshape(rows, width)
    supplied = (
        jnp.dot(flat, w_supply, preferred_element_type=jnp.float32)
        .astype(jnp.bfloat16)
        .reshape(months, firms, width)
    )
    extended = padded(supplied, (("firm", 1),), firms)
    tiles = supply_counts.reshape(months, firms, 3 * firms).astype(jnp.bfloat16)
    degree = 1.0 + jnp.sum(supply_counts, axis=(2, 3)).astype(jnp.float32)
    message = jnp.einsum("mfs,msd->mfd", tiles, extended, preferred_element_type=jnp.float32)
    message = message * lax.rsqrt(degree)[..., None]
    bank_local = bank_table.shape[0]
    sector_local = sector_table.shape[0]
    per_owner = bank_local + sector_local
    hub_local = jnp.concatenate([bank_table, sector_table], axis=0)
    bank_flat = bank_ids.reshape(rows)
    sector_flat = sector_ids.reshape(rows)
    bank_pos = bank_flat // bank_local * per_owner + bank_flat % bank_local
    sector_pos = sector_flat // sector_local * per_owner + bank_local + sector_flat % sector_local
    hub_whole = lax.all_gather(hub_local, "firm", axis=0, tiled=True)
    hubs = jnp.take(hub_whole, bank_pos, axis=0).astype(jnp.float32) + jnp.take(
        hub_whole, sector_pos, axis=0
    ).astype(jnp.float32)
    mixed = flat.astype(jnp.float32) + message.reshape(rows, width) + hubs
    normed = rms_norm(mixed, gain_mix).astype(jnp.bfloat16)
    query = (
        jnp.dot(normed, w_query, preferred_element_type=jnp.float32)
        .astype(jnp.bfloat16)
        .reshape(months, firms, width)
    )
    key = (
        jnp.dot(normed, w_key, preferred_element_type=jnp.float32)
        .astype(jnp.bfloat16)
        .reshape(months, firms, width)
    )
    value = (
        jnp.dot(normed, w_value, preferred_element_type=jnp.float32)
        .astype(jnp.bfloat16)
        .reshape(months, firms, width)
    )
    earlier_key, earlier_value = from_behind((key, value), "tm", 1)
    earlier_key = earlier_key[months - 3 :]
    earlier_value = earlier_value[months - 3 :]
    keys_all = jnp.concatenate([earlier_key, key], axis=0)
    values_all = jnp.concatenate([earlier_value, value], axis=0)
    heads = HEADS
    head_size = width // heads
    query4 = query.reshape(months, firms, heads, head_size)
    first_month = lax.axis_index("tm") * months
    month_local = lax.iota(jnp.int32, months)
    total = jnp.zeros((months, firms, heads, head_size), jnp.float32)
    for lag in range(4):
        key_l = keys_all[3 - lag : 3 - lag + months].reshape(months, firms, heads, head_size)
        value_l = values_all[3 - lag : 3 - lag + months].reshape(months, firms, heads, head_size)
        score = jnp.einsum(
            "mfhd,mfhd->mfh", query4, key_l, preferred_element_type=jnp.float32
        ) / jnp.sqrt(jnp.float32(head_size)) - jnp.log(jnp.float32(4.0))
        valid = (first_month + month_local - lag >= 0).astype(jnp.float32)[:, None, None]
        total = total + (jax.nn.sigmoid(score) * valid)[..., None] * value_l.astype(jnp.float32)
    attended = total.astype(jnp.bfloat16).reshape(rows, width)
    second = mixed + jnp.dot(attended, w_out, preferred_element_type=jnp.float32)
    normed2 = rms_norm(second, gain_ffn).astype(jnp.bfloat16)
    inner = jax.nn.gelu(jnp.dot(normed2, w_in, preferred_element_type=jnp.float32)).astype(
        jnp.bfloat16
    )
    final = second + jnp.dot(inner, w_down, preferred_element_type=jnp.float32)
    return final.astype(jnp.bfloat16).reshape(months, firms, width)


def solution(mesh):
    in_specs = (
        P("tm", "firm", None),
        P("tm", "firm", None, None),
        P("tm", "firm"),
        P("tm", "firm"),
        P("firm", None),
        P("firm", None),
        P(),
        P(),
        P(),
        P(),
        P(),
        P(),
        P(),
        P(),
        P(),
    )
    out_specs = P("tm", "firm", None)
    return jax.shard_map(body, mesh=mesh, in_specs=in_specs, out_specs=out_specs, check_vma=False)
```

profile of v0, /device:TPU:1, one launch (start us, length us, event | category | flops | bytes accessed | tf_op | source)
XLA Modules:
  0.0 347.4 jit_solution(13643477030206423323)
XLA Ops:
  0.0 1.7 convolution_convert_fusion.3
  1.8 1.3 collective-permute-start.1
  3.1 7.4 %collective-permute-start = (bf16[8,256,256]{2,1,0:T(8,128)(2,1)S(1)}, bf16[8,256,256]{2,1,0:T(8,128)(2,1)}, u32[]{:S(2)}, u32[]{:S(2)}) collective-permute-start(bf16[8,256,256]{2,1,0:T(8,128)(2,1)S(1)} %bitcast.95), channel_id=1, source_target_pairs={{0,1},{1,2},{2,3},{3,4},{4,5},{5,6},{6,7},{7,8},{8,9},{9,10},{10,1... | collective-permute-start | bytes 3145736 | tf_op jit(solution)/shard_map/ppermute | solution.py:16
  10.4 198.2 %all-gather = bf16[64,12,256]{2,1,0:T(8,128)(2,1)S(1)} all-gather(bf16[1,12,256]{2,1,0:T(8,128)(2,1)S(1)} %maximum_bitcast_fusion), channel_id=1, replica_groups=mesh['tm'=4,'firm'=64] {'firm'}, dimensions={0}, use_global_device_ids=true | all-gather | bytes 399360 | tf_op jit(solution)/shard_map/all_gather | solution.py:71
  208.6 6.6 %copy.26 = s32[8,256,3,256]{1,3,2,0:T(8,128)} copy(s32[8,256,3,256]{3,1,2,0:T(8,128)} %param.18) | data formatting | bytes 12582912 | tf_op args[1]
  215.2 3.1 reduce_sum.27
  218.3 0.1 reshape.138
  218.5 9.1 %gather_fusion.1 = bf16[2048,256]{1,0:T(8,128)(2,1)} fusion(bf16[768,256]{1,0:T(8,128)(2,1)S(1)} %reshape.138, s32[2048]{0:T(1024)S(1)} %broadcast_clamp_fusion), kind=kCustom, calls=%fused_computation.1.clone | custom fusion | bytes 2105344 | tf_op jit(solution)/shard_map/jit(_take)/gather | solution.py:72
  227.6 9.0 %gather_fusion = bf16[2048,256]{1,0:T(8,128)(2,1)} fusion(bf16[768,256]{1,0:T(8,128)(2,1)S(1)} %reshape.138, s32[2048]{0:T(1024)S(1)} %broadcast_clamp_fusion.1), kind=kCustom, calls=%fused_computation.clone | custom fusion | bytes 2105344 | tf_op jit(solution)/shard_map/jit(_take)/gather | solution.py:72
  236.6 5.2 %convert_element_type.105 = bf16[8,256,3,256]{1,3,2,0:T(8,128)(2,1)} convert(s32[8,256,3,256]{1,3,2,0:T(8,128)} %copy.26) | non-fusion elementwise | flops 1572864 | bytes 9437184 | tf_op jit(solution)/shard_map/convert_element_type | solution.py:59
  241.7 0.0 collective-permute-done.1
  241.7 0.0 collective-permute-done
  241.8 0.0 copy-start.7
  241.8 0.0 copy-start.8
  241.8 3.8 %fusion.29 = f32[8,256,256]{1,2,0:T(8,128)S(1)} fusion(bf16[8,256,768]{1,2,0:T(8,128)(2,1)} %bitcast.93, bf16[8,256,256]{2,1,0:T(8,128)(2,1)} %collective-permute-done.1, bf16[8,256,256]{2,1,0:T(8,128)(2,1)S(1)} %bitcast.96, bf16[8,256,256]{2,1,0:T(8,128)(2,1)} %collective-permute-done, f32[8,256]{1,0:T(8,128)S(1)} %add_rsqrt_fusion.2), kind=kOutput, calls=%fused_computation.47 | convolution fusion | flops 815267840 | bytes 8396800 | tf_op jit(solution)/shard_map/mfs,msd->mfd/dot_general | solution.py:61
  245.7 0.0 copy-start.18
  245.7 2.1 multiply_reduce_fusion.5
  247.8 0.0 copy-start.11
  247.8 0.3 multiply_convert_fusion.3
  248.2 0.0 copy-start.1
  248.2 1.0 copy-done.1
  249.2 1.4 convolution_convert_fusion.1
  250.6 2.3 copy.31
  252.9 38.6 %collective-permute-start.2 = (bf16[8,256,256]{1,2,0:T(8,128)(2,1)}, bf16[8,256,256]{1,2,0:T(8,128)(2,1)}, u32[]{:S(2)}, u32[]{:S(2)}) collective-permute-start(bf16[8,256,256]{1,2,0:T(8,128)(2,1)} %copy.31), channel_id=1, source_target_pairs={{0,64},{64,128},{128,192},{1,65},{65,129},{129,193},{2,66},{66,130... | collective-permute-start | bytes 3145736 | tf_op jit(solution)/shard_map/ppermute | solution.py:25
  291.6 2.3 copy.29
  293.8 2.7 convolution_convert_fusion.2
  296.5 2.3 copy.28
  298.8 1.6 copy.59
  300.4 0.3 copy.60
  300.7 0.0 copy-start.2
  300.7 0.0 copy-start.13
  300.7 1.5 convert.11
  302.2 0.0 copy-done.13
  302.3 1.4 convolution_convert_fusion
  303.7 2.1 collective-permute-start.3
  305.8 0.3 multiply_reduce_fusion.3
  306.0 0.1 divide_multiply_fusion
  306.1 0.1 mul.168
  306.3 2.2 copy.61
  308.5 2.9 copy.30
  311.4 0.0 collective-permute-done.2
  311.4 1.0 slice.36
  312.4 2.2 fusion.34
  314.6 0.1 copy-done.3
  314.7 1.4 multiply_reduce_fusion.2
  316.1 0.1 fusion.52
  316.2 0.1 mul.178
  316.3 2.2 copy.63
  318.5 2.9 copy.34
  321.4 0.1 fusion.46
  321.5 0.1 mul.183
  321.7 2.2 copy.64
  323.9 2.9 copy.35
  326.8 0.1 fusion.58
  326.8 0.1 mul.173
  327.0 2.2 copy.62
  329.2 2.9 copy.33
  332.2 1.0 slice.39
  333.2 0.0 copy-start.10
  333.2 2.0 fusion.33
  335.3 0.2 copy-done.4
  335.5 0.6 copy-done.5
  336.1 4.9 %multiply_reduce_fusion.4 = (f32[2048]{0:T(1024)S(1)}, f32[2048,256]{1,0:T(8,128)}) fusion(f32[2048,256]{1,0:T(8,128)S(1)} %get-tuple-element.10, bf16[256,256]{1,0:T(8,128)(2,1)S(1)} %copy-done.10, f32[2048,256]{1,0:T(8,128)} %copy.35, bf16[2048,256]{1,0:T(8,128)(2,1)S(1)} %bitcast.91, f32[2048,256]{1,0:T(8,128)S(1)} %copy-done.5, ...), kind=kOutput, calls=%fused_computation.40 | convolution fusion | flops 276297728 | bytes 16916480 | tf_op jit(solution)/shard_map/dot_general | solution.py:112
  341.1 6.4 %fusion.21 = bf16[2048,256]{1,0:T(8,128)(2,1)} fusion(f32[2048,256]{1,0:T(8,128)} %get-tuple-element.22, bf16[1024,256]{1,0:T(8,128)(2,1)S(1)} %copy-done, bf16[256,1024]{1,0:T(8,128)(2,1)S(1)} %copy-done.19, f32[256]{0:T(256)S(1)} %copy-done.20, f32[2048]{0:T(1024)S(1)} %add_rsqrt_fusion), kind=kOutput, calls=%fused_computation.21 | convolution fusion | flops 2168979456 | bytes 4203520 | tf_op jit(solution)/shard_map/dot_general | solution.py:117
  (41 shorter events, 0.1 us)
Async XLA Ops:
  0.0 341.1 %copy-start = (bf16[1024,256]{1,0:T(8,128)(2,1)S(1)}, bf16[1024,256]{1,0:T(8,128)(2,1)}, u32[]{:S(2)}) copy-start(bf16[1024,256]{1,0:T(8,128)(2,1)} %param.29) | copy-start | bytes 1572868
  0.0 10.4 %copy-start.17 = (bf16[4,256]{1,0:T(4,128)(2,1)S(1)}, bf16[4,256]{1,0:T(4,128)(2,1)}, u32[]{:S(2)}) copy-start(bf16[4,256]{1,0:T(4,128)(2,1)} %param.22) | copy-start | bytes 6148
  0.0 10.4 %copy-start.16 = (bf16[8,256]{1,0:T(8,128)(2,1)S(1)}, bf16[8,256]{1,0:T(8,128)(2,1)}, u32[]{:S(2)}) copy-start(bf16[8,256]{1,0:T(8,128)(2,1)} %param.21) | copy-start | bytes 12292
  0.0 208.6 %copy-start.14 = (s32[8,256]{1,0:T(8,128)S(1)}, s32[8,256]{1,0:T(8,128)}, u32[]{:S(2)}) copy-start(s32[8,256]{1,0:T(8,128)} %param.19) | copy-start | bytes 24580
  0.0 208.6 %copy-start.15 = (s32[8,256]{1,0:T(8,128)S(1)}, s32[8,256]{1,0:T(8,128)}, u32[]{:S(2)}) copy-start(s32[8,256]{1,0:T(8,128)} %param.20) | copy-start | bytes 24580
  1.8 240.0 %collective-permute-start.1 = (bf16[8,256,256]{2,1,0:T(8,128)(2,1)S(1)}, bf16[8,256,256]{2,1,0:T(8,128)(2,1)}, u32[]{:S(2)}, u32[]{:S(2)}) collective-permute-start(bf16[8,256,256]{2,1,0:T(8,128)(2,1)S(1)} %bitcast.94), channel_id=1, source_target_pairs={{1,0},{2,1},{3,2},{4,3},{5,4},{6,5},{7,6},{8,7},{9,8},{10,9},{11,1... | collective-permute-start | bytes 3145736 | tf_op jit(solution)/shard_map/ppermute | solution.py:17
  3.1 238.7 %collective-permute-start = (bf16[8,256,256]{2,1,0:T(8,128)(2,1)S(1)}, bf16[8,256,256]{2,1,0:T(8,128)(2,1)}, u32[]{:S(2)}, u32[]{:S(2)}) collective-permute-start(bf16[8,256,256]{2,1,0:T(8,128)(2,1)S(1)} %bitcast.95), channel_id=1, source_target_pairs={{0,1},{1,2},{2,3},{3,4},{4,5},{5,6},{6,7},{7,8},{8,9},{9,10},{10,1... | collective-permute-start | bytes 3145736 | tf_op jit(solution)/shard_map/ppermute | solution.py:16
  241.8 3.9 %copy-start.7 = (bf16[8,256,256]{2,1,0:T(8,128)(2,1)S(1)}, bf16[8,256,256]{2,1,0:T(8,128)(2,1)}, u32[]{:S(2)}) copy-start(bf16[8,256,256]{2,1,0:T(8,128)(2,1)} %param.17) | copy-start | bytes 3145732
  241.8 3.9 %copy-start.8 = (bf16[2048,256]{1,0:T(8,128)(2,1)S(1)}, bf16[2048,256]{1,0:T(8,128)(2,1)}, u32[]{:S(2)}) copy-start(bf16[2048,256]{1,0:T(8,128)(2,1)} %gather_fusion.1) | copy-start | bytes 3145732
  241.8 3.9 %copy-start.9 = (bf16[2048,256]{1,0:T(8,128)(2,1)S(1)}, bf16[2048,256]{1,0:T(8,128)(2,1)}, u32[]{:S(2)}) copy-start(bf16[2048,256]{1,0:T(8,128)(2,1)} %gather_fusion) | copy-start | bytes 3145732
  245.7 2.2 copy-start.18
  247.8 1.4 copy-start.11
  248.2 1.0 copy-start.1
  250.6 43.2 %copy-start.12 = (bf16[256,256]{1,0:T(8,128)(2,1)S(1)}, bf16[256,256]{1,0:T(8,128)(2,1)}, u32[]{:S(2)}) copy-start(bf16[256,256]{1,0:T(8,128)(2,1)} %param.24) | copy-start | bytes 393220
  252.9 58.5 %collective-permute-start.2 = (bf16[8,256,256]{1,2,0:T(8,128)(2,1)}, bf16[8,256,256]{1,2,0:T(8,128)(2,1)}, u32[]{:S(2)}, u32[]{:S(2)}) collective-permute-start(bf16[8,256,256]{1,2,0:T(8,128)(2,1)} %copy.31), channel_id=1, source_target_pairs={{0,64},{64,128},{128,192},{1,65},{65,129},{129,193},{2,66},{66,130... | collective-permute-start | bytes 3145736 | tf_op jit(solution)/shard_map/ppermute | solution.py:25
  298.8 1.6 copy-start.6
  300.7 1.5 copy-start.2
  300.7 1.5 copy-start.13
  303.7 28.5 %collective-permute-start.3 = (bf16[8,256,256]{2,1,0:T(8,128)(2,1)}, bf16[8,256,256]{2,1,0:T(8,128)(2,1)}, u32[]{:S(2)}, u32[]{:S(2)}) collective-permute-start(bf16[8,256,256]{2,1,0:T(8,128)(2,1)} %bitcast.8), channel_id=1, source_target_pairs={{0,64},{64,128},{128,192},{1,65},{65,129},{129,193},{2,66},{66,130... | collective-permute-start | bytes 3145736 | tf_op jit(solution)/shard_map/ppermute | solution.py:25
  312.4 2.3 copy-start.3
  333.2 2.3 copy-start.4
  333.2 2.9 copy-start.5
  333.2 2.9 copy-start.10
  336.1 4.9 %copy-start.19 = (bf16[256,1024]{1,0:T(8,128)(2,1)S(1)}, bf16[256,1024]{1,0:T(8,128)(2,1)}, u32[]{:S(2)}) copy-start(bf16[256,1024]{1,0:T(8,128)(2,1)} %param.28) | copy-start | bytes 1572868
  336.1 4.9 %copy-start.20 = (f32[256]{0:T(256)S(1)}, f32[256]{0:T(256)}, u32[]{:S(2)}) copy-start(f32[256]{0:T(256)} %param.31) | copy-start | bytes 3076
where the time goes:
time: 348 us; the launch traced here: 347 us
  blocking collectives  198 us (57%)
  local copies, waits for them, and re-layouts  58.7 us (17%)
  starting transfers between devices  49.4 us (14%)
  matrix products  22.3 us (6%)
  other arithmetic  18.5 us (5%)
    all_gather x1, blocking collectives, body(): hub_whole = lax.all_gather(hub_local, 'firm', axis=0, tiled=True)  198 us
    ppermute x2, starting transfers between devices, from_behind(): return lax.ppermute(x, axis, pairs)  40.7 us
    unnamed x52, local copies, waits for them, and re-layouts  19.5 us
    mul x8, local copies, waits for them, and re-layouts, body(): (jax.nn.sigmoid(score) * valid)[..., None] * value_l.astype(jnp.float32)  12.2 us
    gather x1, local copies, waits for them, and re-layouts, body(): jnp.take(hub_whole, sector_pos, axis=0).astype(jnp.float32)  9.06 us
    gather x1, local copies, waits for them, and re-layouts, body(): jnp.take(hub_whole, bank_pos, axis=0).astype(jnp.float32)  9 us
    ppermute x1, starting transfers between devices, padded(): before = lax.ppermute(last, axis, up)  7.35 us
  transfers between devices with their start and end apart: 4, of which 0 were waited for; matrix products, arithmetic and copies ran while one was open for 21% of the time, Pallas kernels for 0%

commit v1 on v0

--- a/solution.py
+++ b/solution.py
@@ -68,7 +68,9 @@
     sector_flat = sector_ids.reshape(rows)
     bank_pos = bank_flat // bank_local * per_owner + bank_flat % bank_local
     sector_pos = sector_flat // sector_local * per_owner + bank_local + sector_flat % sector_local
-    hub_whole = lax.all_gather(hub_local, "firm", axis=0, tiled=True)
+    hub_whole = jnp.concatenate(
+        lax.all_to_all(jnp.stack([hub_local] * lax.axis_size("firm")), "firm", 0, 0), axis=0
+    )
     hubs = jnp.take(hub_whole, bank_pos, axis=0).astype(jnp.float32) + jnp.take(
         hub_whole, sector_pos, axis=0
     ).astype(jnp.float32)

time: 348 us -> 171 us (0.49)
  blocking collectives: 198 us -> 0 us
  waiting for transfers between devices: 0.01 us -> 35.6 us
  starting transfers between devices: 49.4 us -> 33.7 us
    all_gather x1 -> x0, blocking collectives: 198 us -> none  [body(): hub_whole = lax.all_gather(hub_local, 'firm', axis=0, tiled=True)]
    all_to_all x0 -> x1, waiting for transfers between devices: none -> 35.6 us  [body(): lax.all_to_all(jnp.stack([hub_local] * lax.axis_size('firm')), 'firm', 0, 0)]
    ppermute x2, starting transfers between devices: 40.7 us -> 9.36 us  [from_behind(): return lax.ppermute(x, axis, pairs)]
    all_to_all x0 -> x1, starting transfers between devices: none -> 15.7 us  [body(): lax.all_to_all(jnp.stack([hub_local] * lax.axis_size('firm')), 'firm', 0, 0)]
    unnamed x52 -> x51, local copies, waits for them, and re-layouts: 19.5 us -> 19.5 us
  transfers between devices with their start and end apart: 4 -> 5, of which waited for: 0 -> 1; matrix products, arithmetic and copies ran while one was open for 21% -> 42% of each run, Pallas kernels for 0% -> 0%
where the time goes in v1:
time: 171 us; the launch traced here: 170 us
  local copies, waits for them, and re-layouts  59.6 us (35%)
  waiting for transfers between devices  35.6 us (21%)
  starting transfers between devices  33.7 us (20%)
  matrix products  22.4 us (13%)
  other arithmetic  18.5 us (11%)
    all_to_all x1, waiting for transfers between devices, body(): lax.all_to_all(jnp.stack([hub_local] * lax.axis_size('firm')), 'firm', 0, 0)  35.6 us
    unnamed x51, local copies, waits for them, and re-layouts  19.5 us
    all_to_all x1, starting transfers between devices, body(): lax.all_to_all(jnp.stack([hub_local] * lax.axis_size('firm')), 'firm', 0, 0)  15.7 us
    mul x8, local copies, waits for them, and re-layouts, body(): (jax.nn.sigmoid(score) * valid)[..., None] * value_l.astype(jnp.float32)  12.2 us
    ppermute x2, starting transfers between devices, from_behind(): return lax.ppermute(x, axis, pairs)  9.36 us
    gather x1, local copies, waits for them, and re-layouts, body(): jnp.take(hub_whole, sector_pos, axis=0).astype(jnp.float32)  9.06 us
    gather x1, local copies, waits for them, and re-layouts, body(): jnp.take(hub_whole, bank_pos, axis=0).astype(jnp.float32)  9.04 us
    ppermute x1, starting transfers between devices, padded(): before = lax.ppermute(last, axis, up)  7.35 us
  transfers between devices with their start and end apart: 5, of which 1 were waited for; matrix products, arithmetic and copies ran while one was open for 42% of the time, Pallas kernels for 0%

profile of v1, /device:TPU:1, one launch (start us, length us, event | category | flops | bytes accessed | tf_op | source)
XLA Modules:
  0.0 170.3 jit_solution(9834215630692975123)
XLA Ops:
  0.0 1.7 %convolution_convert_fusion.3 = bf16[2048,256]{1,0:T(8,128)(2,1)S(1)} fusion(bf16[2048,256]{1,0:T(8,128)(2,1)} %bitcast.87, bf16[256,256]{1,0:T(8,128)(2,1)} %param.23), kind=kOutput, calls=%fused_computation.25 | convolution fusion | flops 268959744 | bytes 2228224 | tf_op jit(solution)/shard_map/dot_general | solution.py:54
  1.8 1.3 collective-permute-start.1
  3.1 7.3 %collective-permute-start = (bf16[8,256,256]{2,1,0:T(8,128)(2,1)S(1)}, bf16[8,256,256]{2,1,0:T(8,128)(2,1)}, u32[]{:S(2)}, u32[]{:S(2)}) collective-permute-start(bf16[8,256,256]{2,1,0:T(8,128)(2,1)S(1)} %bitcast.93), channel_id=1, source_target_pairs={{0,1},{1,2},{2,3},{3,4},{4,5},{5,6},{6,7},{7,8},{8,9},{9,10},{10,1... | collective-permute-start | bytes 3145736 | tf_op jit(solution)/shard_map/ppermute | solution.py:16
  10.4 0.8 stack.2
  11.2 15.7 %all-to-all-start = ((bf16[64,12,256]{2,1,0:T(8,128)(2,1)}), bf16[64,12,256]{2,1,0:T(8,128)(2,1)S(1)}, u32[]{:S(2)}, u32[]{:S(2)}) async-start(bf16[64,12,256]{2,1,0:T(8,128)(2,1)} %stack.2), calls=%async_computation | async-start | bytes 1048576 | tf_op jit(solution)/shard_map/all_to_all | solution.py:72
  27.0 6.6 %copy.16 = s32[8,256,3,256]{1,3,2,0:T(8,128)} copy(s32[8,256,3,256]{3,1,2,0:T(8,128)} %param.18) | data formatting | bytes 12582912 | tf_op args[1]
  33.6 3.1 %reduce_sum.27 = s32[8,256]{1,0:T(8,128)S(1)} reduce(s32[8,256,3,256]{3,1,2,0:T(8,128)} %param.18, s32[]{:T(128)} %constant.84.clone.1), dimensions={2,3}, to_apply=%region_0.0 | reduce | flops 1570816 | bytes 6299652 | tf_op jit(solution)/shard_map/reduce_sum | solution.py:60
  36.8 5.2 %convert_element_type.105 = bf16[8,256,3,256]{1,3,2,0:T(8,128)(2,1)} convert(s32[8,256,3,256]{1,3,2,0:T(8,128)} %copy.16) | non-fusion elementwise | flops 1572864 | bytes 9437184 | tf_op jit(solution)/shard_map/convert_element_type | solution.py:59
  42.0 35.6 %all-to-all-done = bf16[64,12,256]{2,1,0:T(8,128)(2,1)S(1)} async-done(((bf16[64,12,256]{2,1,0:T(8,128)(2,1)}), bf16[64,12,256]{2,1,0:T(8,128)(2,1)S(1)}, u32[]{:S(2)}, u32[]{:S(2)}) %all-to-all-start) | async-done | bytes 393248 | tf_op jit(solution)/shard_map/all_to_all | solution.py:72
  77.6 0.1 reshape.113
  77.7 9.1 %gather_fusion.1 = bf16[2048,256]{1,0:T(8,128)(2,1)} fusion(bf16[768,256]{1,0:T(8,128)(2,1)S(1)} %reshape.113, s32[2048]{0:T(1024)S(1)} %broadcast_clamp_fusion), kind=kCustom, calls=%fused_computation.1.clone | custom fusion | bytes 2105344 | tf_op jit(solution)/shard_map/jit(_take)/gather | solution.py:74
  86.8 9.0 %gather_fusion = bf16[2048,256]{1,0:T(8,128)(2,1)} fusion(bf16[768,256]{1,0:T(8,128)(2,1)S(1)} %reshape.113, s32[2048]{0:T(1024)S(1)} %broadcast_clamp_fusion.1), kind=kCustom, calls=%fused_computation.clone | custom fusion | bytes 2105344 | tf_op jit(solution)/shard_map/jit(_take)/gather | solution.py:74
  95.8 0.0 copy-start.8
  95.9 3.8 %fusion.29 = f32[8,256,256]{1,2,0:T(8,128)S(1)} fusion(bf16[8,256,768]{1,2,0:T(8,128)(2,1)} %bitcast.91, bf16[8,256,256]{2,1,0:T(8,128)(2,1)} %collective-permute-done.1, bf16[8,256,256]{2,1,0:T(8,128)(2,1)S(1)} %bitcast.94, bf16[8,256,256]{2,1,0:T(8,128)(2,1)} %collective-permute-done, f32[8,256]{1,0:T(8,128)S(1)} %add_rsqrt_fusion.2), kind=kOutput, calls=%fused_computation.47 | convolution fusion | flops 815267840 | bytes 8396800 | tf_op jit(solution)/shard_map/mfs,msd->mfd/dot_general | solution.py:61
  99.7 0.0 copy-start.18
  99.8 2.1 %multiply_reduce_fusion.5 = (f32[2048]{0:T(1024)S(1)}, f32[2048,256]{1,0:T(8,128)S(1)}) fusion(bf16[2048,256]{1,0:T(8,128)(2,1)S(1)} %copy-done.8, pred[2048]{0:T(1024)(128)(4,1)S(1)} %get-tuple-element.13, bf16[2048,256]{1,0:T(8,128)(2,1)S(1)} %copy-done.9, pred[2048]{0:T(1024)(128)(4,1)S(1)} %get-tuple-element.23, f32[8,256,256]{1,2,0:T(8,128)S(1)} %fusion.29, ...), kind=kLoop, calls=%fused_computation.42 | loop fusion | flops 5240832 | bytes 7352320 | tf_op jit(solution)/shard_map/reduce_sum | solution.py:29
  101.9 0.0 copy-start.11
  101.9 0.3 multiply_convert_fusion.3
  102.3 0.0 copy-start.1
  102.3 1.0 copy-done.1
  103.2 1.4 convolution_convert_fusion.1
  104.7 2.3 %copy.21 = bf16[8,256,256]{1,2,0:T(8,128)(2,1)} copy(bf16[8,256,256]{2,1,0:T(8,128)(2,1)} %bitcast.75) | data formatting | bytes 2097152 | tf_op jit(solution)/shard_map/reshape | solution.py:87
  107.0 7.3 %collective-permute-start.2 = (bf16[8,256,256]{1,2,0:T(8,128)(2,1)}, bf16[8,256,256]{1,2,0:T(8,128)(2,1)}, u32[]{:S(2)}, u32[]{:S(2)}) collective-permute-start(bf16[8,256,256]{1,2,0:T(8,128)(2,1)} %copy.21), channel_id=1, source_target_pairs={{0,64},{64,128},{128,192},{1,65},{65,129},{129,193},{2,66},{66,130... | collective-permute-start | bytes 3145736 | tf_op jit(solution)/shard_map/ppermute | solution.py:25
  114.3 2.3 %copy.19 = bf16[2048,256]{0,1:T(8,128)(2,1)} copy(bf16[2048,256]{1,0:T(8,128)(2,1)} %convolution_convert_fusion.1) | data formatting | bytes 2097152 | tf_op jit(solution)/shard_map/convert_element_type | solution.py:86
  116.5 2.7 %convolution_convert_fusion.2 = bf16[2048,256]{1,0:T(8,128)(2,1)} fusion(bf16[2048,256]{1,0:T(8,128)(2,1)} %copy-done.1, bf16[256,256]{1,0:T(8,128)(2,1)S(1)} %copy-done.12), kind=kOutput, calls=%fused_computation.24 | convolution fusion | flops 268959744 | bytes 2228224 | tf_op jit(solution)/shard_map/dot_general | solution.py:80
  119.2 2.3 %copy.18 = bf16[2048,256]{0,1:T(8,128)(2,1)} copy(bf16[2048,256]{1,0:T(8,128)(2,1)} %convolution_convert_fusion.2) | data formatting | bytes 2097152 | tf_op jit(solution)/shard_map/convert_element_type | solution.py:81
  121.5 1.6 copy.49
  123.1 0.3 copy.50
  123.4 0.0 copy-start.2
  123.4 0.0 copy-start.13
  123.4 1.5 convert.11
  124.9 0.0 copy-done.13
  125.0 1.4 convolution_convert_fusion
  126.4 2.1 %collective-permute-start.3 = (bf16[8,256,256]{2,1,0:T(8,128)(2,1)}, bf16[8,256,256]{2,1,0:T(8,128)(2,1)}, u32[]{:S(2)}, u32[]{:S(2)}) collective-permute-start(bf16[8,256,256]{2,1,0:T(8,128)(2,1)} %bitcast.7), channel_id=1, source_target_pairs={{0,64},{64,128},{128,192},{1,65},{65,129},{129,193},{2,66},{66,130... | collective-permute-start | bytes 3145736 | tf_op jit(solution)/shard_map/ppermute | solution.py:25
  128.5 0.3 multiply_reduce_fusion.3
  128.8 0.1 divide_multiply_fusion
  128.8 0.1 mul.168
  129.0 2.2 %copy.51 = f32[32,8,8,256]{3,1,2,0:T(8,128)} copy(f32[32,8,8,256]{3,2,1,0:T(8,128)S(1)} %bitcast.76) | data formatting | bytes 4194304
  131.2 2.9 %copy.20 = f32[2048,256]{1,0:T(8,128)} copy(f32[2048,256]{0,1:T(8,128)} %bitcast.77) | data formatting | bytes 4194304 | tf_op jit(solution)/shard_map/mul | solution.py:112
  134.1 0.0 collective-permute-done.2
  134.1 1.0 slice.36
  135.1 2.1 %fusion.34 = (bf16[8,256,256]{1,2,0:T(8,128)(2,1)S(1)}, bf16[8,256,256]{1,2,0:T(8,128)(2,1)S(1)}, bf16[8,256,256]{1,2,0:T(8,128)(2,1)S(1)}) fusion(bf16[8,256,256]{1,2,0:T(8,128)(2,1)} %copy.21, bf16[3,256,256]{1,2,0:T(8,128)(2,1)S(1)} %slice.36), kind=kLoop, calls=%fused_computation.54 | loop fusion | flops 1572864 | bytes 4587520 | tf_op jit(solution)/shard_map/concatenate | solution.py:97
  137.3 0.2 copy-done.3
  137.4 1.4 multiply_reduce_fusion.2
  138.8 0.1 fusion.52
  138.9 0.1 mul.178
  139.1 2.2 %copy.53 = f32[32,8,8,256]{3,1,2,0:T(8,128)} copy(f32[32,8,8,256]{3,2,1,0:T(8,128)S(1)} %bitcast.78) | data formatting | bytes 4194304
  141.3 2.9 %copy.24 = f32[2048,256]{1,0:T(8,128)} copy(f32[2048,256]{0,1:T(8,128)} %bitcast.79) | data formatting | bytes 4194304 | tf_op jit(solution)/shard_map/mul | solution.py:112
  144.2 0.1 fusion.46
  144.2 0.1 mul.183
  144.4 2.2 %copy.54 = f32[32,8,8,256]{3,1,2,0:T(8,128)} copy(f32[32,8,8,256]{3,2,1,0:T(8,128)S(1)} %bitcast.80) | data formatting | bytes 4194304
  146.6 2.9 %copy.25 = f32[2048,256]{1,0:T(8,128)} copy(f32[2048,256]{0,1:T(8,128)} %bitcast.81) | data formatting | bytes 4194304 | tf_op jit(solution)/shard_map/mul | solution.py:112
  149.5 0.1 fusion.58
  149.6 0.1 mul.173
  149.8 2.2 %copy.52 = f32[32,8,8,256]{3,1,2,0:T(8,128)} copy(f32[32,8,8,256]{3,2,1,0:T(8,128)S(1)} %bitcast.82) | data formatting | bytes 4194304
  152.0 2.9 %copy.23 = f32[2048,256]{1,0:T(8,128)} copy(f32[2048,256]{0,1:T(8,128)} %bitcast.83) | data formatting | bytes 4194304 | tf_op jit(solution)/shard_map/mul | solution.py:112
  154.9 0.0 collective-permute-done.3
  154.9 1.0 slice.39
  156.0 0.0 copy-start.10
  156.0 2.0 %fusion.33 = (bf16[8,256,256]{2,1,0:T(8,128)(2,1)S(1)}, bf16[8,256,256]{2,1,0:T(8,128)(2,1)S(1)}, bf16[8,256,256]{2,1,0:T(8,128)(2,1)S(1)}) fusion(bf16[8,256,256]{2,1,0:T(8,128)(2,1)} %bitcast.7, bf16[3,256,256]{2,1,0:T(8,128)(2,1)S(1)} %slice.39), kind=kLoop, calls=%fused_computation.53 | loop fusion | flops 1572864 | bytes 4587520 | tf_op jit(solution)/shard_map/concatenate | solution.py:98
  158.0 0.2 copy-done.4
  158.3 0.6 copy-done.5
  158.9 4.9 %multiply_reduce_fusion.4 = (f32[2048]{0:T(1024)S(1)}, f32[2048,256]{1,0:T(8,128)}) fusion(f32[2048,256]{1,0:T(8,128)S(1)} %get-tuple-element.10, bf16[256,256]{1,0:T(8,128)(2,1)S(1)} %copy-done.10, f32[2048,256]{1,0:T(8,128)} %copy.25, bf16[2048,256]{1,0:T(8,128)(2,1)S(1)} %bitcast.89, f32[2048,256]{1,0:T(8,128)S(1)} %copy-done.5, ...), kind=kOutput, calls=%fused_computation.40 | convolution fusion | flops 276297728 | bytes 16916480 | tf_op jit(solution)/shard_map/dot_general | solution.py:114
  163.9 6.4 %fusion.21 = bf16[2048,256]{1,0:T(8,128)(2,1)} fusion(f32[2048,256]{1,0:T(8,128)} %get-tuple-element.22, bf16[1024,256]{1,0:T(8,128)(2,1)S(1)} %copy-done, bf16[256,1024]{1,0:T(8,128)(2,1)S(1)} %copy-done.19, f32[256]{0:T(256)S(1)} %copy-done.20, f32[2048]{0:T(1024)S(1)} %add_rsqrt_fusion), kind=kOutput, calls=%fused_computation.21 | convolution fusion | flops 2168979456 | bytes 4203520 | tf_op jit(solution)/shard_map/dot_general | solution.py:119
  (43 shorter events, 0.2 us)
Async XLA Ops:
  0.0 163.8 %copy-start = (bf16[1024,256]{1,0:T(8,128)(2,1)S(1)}, bf16[1024,256]{1,0:T(8,128)(2,1)}, u32[]{:S(2)}) copy-start(bf16[1024,256]{1,0:T(8,128)(2,1)} %param.29) | copy-start | bytes 1572868
  0.0 10.4 %copy-start.17 = (bf16[4,256]{1,0:T(4,128)(2,1)S(1)}, bf16[4,256]{1,0:T(4,128)(2,1)}, u32[]{:S(2)}) copy-start(bf16[4,256]{1,0:T(4,128)(2,1)} %param.22) | copy-start | bytes 6148
  0.0 10.4 %copy-start.16 = (bf16[8,256]{1,0:T(8,128)(2,1)S(1)}, bf16[8,256]{1,0:T(8,128)(2,1)}, u32[]{:S(2)}) copy-start(bf16[8,256]{1,0:T(8,128)(2,1)} %param.21) | copy-start | bytes 12292
  0.0 27.0 %copy-start.14 = (s32[8,256]{1,0:T(8,128)S(1)}, s32[8,256]{1,0:T(8,128)}, u32[]{:S(2)}) copy-start(s32[8,256]{1,0:T(8,128)} %param.19) | copy-start | bytes 24580
  0.0 27.0 %copy-start.15 = (s32[8,256]{1,0:T(8,128)S(1)}, s32[8,256]{1,0:T(8,128)}, u32[]{:S(2)}) copy-start(s32[8,256]{1,0:T(8,128)} %param.20) | copy-start | bytes 24580
  1.8 94.1 %collective-permute-start.1 = (bf16[8,256,256]{2,1,0:T(8,128)(2,1)S(1)}, bf16[8,256,256]{2,1,0:T(8,128)(2,1)}, u32[]{:S(2)}, u32[]{:S(2)}) collective-permute-start(bf16[8,256,256]{2,1,0:T(8,128)(2,1)S(1)} %bitcast.92), channel_id=1, source_target_pairs={{1,0},{2,1},{3,2},{4,3},{5,4},{6,5},{7,6},{8,7},{9,8},{10,9},{11,1... | collective-permute-start | bytes 3145736 | tf_op jit(solution)/shard_map/ppermute | solution.py:17
  3.1 92.8 %collective-permute-start = (bf16[8,256,256]{2,1,0:T(8,128)(2,1)S(1)}, bf16[8,256,256]{2,1,0:T(8,128)(2,1)}, u32[]{:S(2)}, u32[]{:S(2)}) collective-permute-start(bf16[8,256,256]{2,1,0:T(8,128)(2,1)S(1)} %bitcast.93), channel_id=1, source_target_pairs={{0,1},{1,2},{2,3},{3,4},{4,5},{5,6},{6,7},{7,8},{8,9},{9,10},{10,1... | collective-permute-start | bytes 3145736 | tf_op jit(solution)/shard_map/ppermute | solution.py:16
  11.2 66.4 %all-to-all-start = ((bf16[64,12,256]{2,1,0:T(8,128)(2,1)}), bf16[64,12,256]{2,1,0:T(8,128)(2,1)S(1)}, u32[]{:S(2)}, u32[]{:S(2)}) async-start(bf16[64,12,256]{2,1,0:T(8,128)(2,1)} %stack.2), calls=%async_computation | async-start | bytes 1048576 | tf_op jit(solution)/shard_map/all_to_all | solution.py:72
  95.8 3.9 %copy-start.7 = (bf16[8,256,256]{2,1,0:T(8,128)(2,1)S(1)}, bf16[8,256,256]{2,1,0:T(8,128)(2,1)}, u32[]{:S(2)}) copy-start(bf16[8,256,256]{2,1,0:T(8,128)(2,1)} %param.17) | copy-start | bytes 3145732
  95.8 3.9 %copy-start.8 = (bf16[2048,256]{1,0:T(8,128)(2,1)S(1)}, bf16[2048,256]{1,0:T(8,128)(2,1)}, u32[]{:S(2)}) copy-start(bf16[2048,256]{1,0:T(8,128)(2,1)} %gather_fusion.1) | copy-start | bytes 3145732
  95.9 3.9 %copy-start.9 = (bf16[2048,256]{1,0:T(8,128)(2,1)S(1)}, bf16[2048,256]{1,0:T(8,128)(2,1)}, u32[]{:S(2)}) copy-start(bf16[2048,256]{1,0:T(8,128)(2,1)} %gather_fusion) | copy-start | bytes 3145732
  99.7 2.2 %copy-start.18 = (f32[256]{0:T(256)S(1)}, f32[256]{0:T(256)}, u32[]{:S(2)}) copy-start(f32[256]{0:T(256)} %param.30) | copy-start | bytes 3076
  101.9 1.4 copy-start.11
  102.3 1.0 copy-start.1
  104.7 11.9 %copy-start.12 = (bf16[256,256]{1,0:T(8,128)(2,1)S(1)}, bf16[256,256]{1,0:T(8,128)(2,1)}, u32[]{:S(2)}) copy-start(bf16[256,256]{1,0:T(8,128)(2,1)} %param.24) | copy-start | bytes 393220
  107.0 27.1 %collective-permute-start.2 = (bf16[8,256,256]{1,2,0:T(8,128)(2,1)}, bf16[8,256,256]{1,2,0:T(8,128)(2,1)}, u32[]{:S(2)}, u32[]{:S(2)}) collective-permute-start(bf16[8,256,256]{1,2,0:T(8,128)(2,1)} %copy.21), channel_id=1, source_target_pairs={{0,64},{64,128},{128,192},{1,65},{65,129},{129,193},{2,66},{66,130... | collective-permute-start | bytes 3145736 | tf_op jit(solution)/shard_map/ppermute | solution.py:25
  121.5 1.6 copy-start.6
  123.4 1.5 copy-start.2
  123.4 1.5 copy-start.13
  126.4 28.6 %collective-permute-start.3 = (bf16[8,256,256]{2,1,0:T(8,128)(2,1)}, bf16[8,256,256]{2,1,0:T(8,128)(2,1)}, u32[]{:S(2)}, u32[]{:S(2)}) collective-permute-start(bf16[8,256,256]{2,1,0:T(8,128)(2,1)} %bitcast.7), channel_id=1, source_target_pairs={{0,64},{64,128},{128,192},{1,65},{65,129},{129,193},{2,66},{66,130... | collective-permute-start | bytes 3145736 | tf_op jit(solution)/shard_map/ppermute | solution.py:25
  135.1 2.3 %copy-start.3 = (f32[8,256,4,64]{1,0,3,2:T(8,128)S(1)}, f32[8,256,4,64]{1,0,3,2:T(8,128)}, u32[]{:S(2)}) copy-start(f32[8,256,4,64]{1,0,3,2:T(8,128)} %convert.11) | copy-start | bytes 6291460
  156.0 2.3 %copy-start.4 = (f32[2048,256]{1,0:T(8,128)S(1)}, f32[2048,256]{1,0:T(8,128)}, u32[]{:S(2)}) copy-start(f32[2048,256]{1,0:T(8,128)} %copy.20) | copy-start | bytes 6291460
  156.0 2.9 %copy-start.5 = (f32[2048,256]{1,0:T(8,128)S(1)}, f32[2048,256]{1,0:T(8,128)}, u32[]{:S(2)}) copy-start(f32[2048,256]{1,0:T(8,128)} %copy.24) | copy-start | bytes 6291460
  156.0 2.9 %copy-start.10 = (bf16[256,256]{1,0:T(8,128)(2,1)S(1)}, bf16[256,256]{1,0:T(8,128)(2,1)}, u32[]{:S(2)}) copy-start(bf16[256,256]{1,0:T(8,128)(2,1)} %param.27) | copy-start | bytes 393220
  158.9 4.9 %copy-start.19 = (bf16[256,1024]{1,0:T(8,128)(2,1)S(1)}, bf16[256,1024]{1,0:T(8,128)(2,1)}, u32[]{:S(2)}) copy-start(bf16[256,1024]{1,0:T(8,128)(2,1)} %param.28) | copy-start | bytes 1572868
  158.9 5.0 %copy-start.20 = (f32[256]{0:T(256)S(1)}, f32[256]{0:T(256)}, u32[]{:S(2)}) copy-start(f32[256]{0:T(256)} %param.31) | copy-start | bytes 3076
